TPU v7x, 256 devices: a whole 4x4x8 slice. The times are simulated.
256 devices in a mesh: wall: 16 (over y, x_lo, core), span: 16 (over x_hi, z).
Axes of the slice: x: 4 (x_hi: 2, x_lo: 2; x = x_hi * 2 + x_lo), y: 4, z: 8, core: 2. Of those that a mesh axis runs over, the one named last changes fastest.
Arguments:
- field: float32 [4, 3, 2, 512, 6144], P(None, None, None, 'wall', 'span'), may hold values from -6 to 6
- mean_flow: float32 [2, 512], P(None, 'wall'), may hold values from 0.2 to 1.5
- d2_coef: float32 [15, 512], P(None, 'wall'), may hold values from -2 to 2
- wall_coef: float32 [2, 8], replicated, may hold values from -0.4375 to 0.4375
- kx_index: int32 [4], replicated, may hold values from 1 to 7
- patch_of: int32 [6144], P('span'), may hold values from 0 to 63
Outputs:
- new_field: float32 [4, 3, 2, 512, 6144], P(None, None, None, 'wall', 'span')
- wall_grad: float32 [2, 4, 2, 64], replicated
All inputs are finite; a program needn't handle non-finite values.
Results may differ from a plain program's by a relative error of at most 0.000073.
Values sent between devices are 32-bit elements; how exact they have to be, the bound alone decides.
A program may use at most 128 MiB of HBM per device.

v0:
```python
import math
import jax
import jax.numpy as jnp
from jax import lax
from jax.sharding import PartitionSpec as P

HALO = 7
STEN = 15
PATCH = 64
TAU = 0.25
VIS = 0.5


def with_halo(block, sides, width):
    for axis, dim in sides:
        count = lax.axis_size(axis)
        forward = [(i, i + 1) for i in range(count - 1)]
        backward = [(target, source) for source, target in forward]
        low = lax.ppermute(
            lax.slice_in_dim(block, block.shape[dim] - width, None, axis=dim), axis, forward
        )
        high = lax.ppermute(lax.slice_in_dim(block, 0, width, axis=dim), axis, backward)
        block = jnp.concatenate([low, block, high], axis=dim)
    return block


def spanwise_operator(line_data):
    item_count, part_count, row_count, length = line_data.shape
    inner_size = 128
    outer_size = length // inner_size
    highest = lax.Precision.HIGHEST
    real_part = line_data[:, 0].reshape(item_count, row_count, outer_size, inner_size)
    imag_part = line_data[:, 1].reshape(item_count, row_count, outer_size, inner_size)
    outer = jnp.arange(outer_size, dtype=jnp.int32)
    inner = jnp.arange(inner_size, dtype=jnp.int32)
    angle_one = (
        -2.0
        * math.pi
        / outer_size
        * (outer[:, None] * outer[None, :] % outer_size).astype(jnp.float32)
    )
    angle_two = (
        -2.0
        * math.pi
        / inner_size
        * (inner[:, None] * inner[None, :] % inner_size).astype(jnp.float32)
    )
    angle_twist = (
        -2.0 * math.pi / length * (outer[:, None] * inner[None, :] % length).astype(jnp.float32)
    )
    cos_one, sin_one = (jnp.cos(angle_one), jnp.sin(angle_one))
    cos_two, sin_two = (jnp.cos(angle_two), jnp.sin(angle_two))
    cos_twist, sin_twist = (jnp.cos(angle_twist), jnp.sin(angle_twist))

    def first_section(table, values):
        return jnp.einsum("kn,irnm->irkm", table, values, precision=highest)

    def second_section(values, table):
        return jnp.einsum("irkn,nm->irkm", values, table, precision=highest)

    def second_back(values, table):
        return jnp.einsum("irkm,nm->irkn", values, table, precision=highest)

    def first_back(table, values):
        return jnp.einsum("kn,irkm->irnm", table, values, precision=highest)

    section_real = first_section(cos_one, real_part) - first_section(sin_one, imag_part)
    section_imag = first_section(cos_one, imag_part) + first_section(sin_one, real_part)
    twist_real = section_real * cos_twist - section_imag * sin_twist
    twist_imag = section_real * sin_twist + section_imag * cos_twist
    modes_real = second_section(twist_real, cos_two) - second_section(twist_imag, sin_two)
    modes_imag = second_section(twist_real, sin_two) + second_section(twist_imag, cos_two)
    wave_index = outer[:, None] + outer_size * inner[None, :]
    signed = jnp.where(wave_index > length // 2, wave_index - length, wave_index)
    cutoff = length // 3
    wave_ratio = signed.astype(jnp.float32) / cutoff
    multiplier = jnp.where(
        jnp.abs(signed) < cutoff, -VIS * wave_ratio * wave_ratio, 0.0 * wave_ratio
    )
    modes_real = modes_real * multiplier
    modes_imag = modes_imag * multiplier
    back_real = second_back(modes_real, cos_two) + second_back(modes_imag, sin_two)
    back_imag = second_back(modes_imag, cos_two) - second_back(modes_real, sin_two)
    untwist_real = back_real * cos_twist + back_imag * sin_twist
    untwist_imag = back_imag * cos_twist - back_real * sin_twist
    result_real = (first_back(cos_one, untwist_real) + first_back(sin_one, untwist_imag)) / length
    result_imag = (first_back(cos_one, untwist_imag) - first_back(sin_one, untwist_real)) / length
    result_real = result_real.reshape(item_count, row_count, length)
    result_imag = result_imag.reshape(item_count, row_count, length)
    return jnp.stack([result_real, result_imag], axis=1)


def on_device(field, mean_flow, d2_coef, wall_coef, kx_index, patch_of):
    mode_count, comp_count, part_count, row_count, col_count = field.shape
    padded = with_halo(field, (("wall", 3),), HALO)
    diffusion = jnp.zeros_like(field)
    for offset in range(STEN):
        diffusion = (
            diffusion + d2_coef[offset][:, None] * padded[:, :, :, offset : offset + row_count, :]
        )
    flattened = field.reshape(mode_count * comp_count, part_count, row_count, col_count)
    spectral_lines = spanwise_operator(
        lax.all_to_all(flattened, "span", split_axis=2, concat_axis=3, tiled=True)
    )
    spanwise = lax.all_to_all(spectral_lines, "span", split_axis=3, concat_axis=2, tiled=True)
    spanwise = spanwise.reshape(field.shape)
    wave_number = kx_index.astype(jnp.float32) * 0.25
    velocity = mean_flow[0]
    shear_rate = mean_flow[1]
    advect_rate = wave_number[:, None, None, None] * velocity[None, None, :, None]
    advect_real = -advect_rate * field[:, :, 1]
    advect_imag = advect_rate * field[:, :, 0]
    advection = jnp.stack([advect_real, advect_imag], axis=2)
    coupling = shear_rate[None, None, :, None] * field[:, 0]
    advection = advection.at[:, 1].add(-coupling)
    new_field = field + TAU * advection + diffusion + spanwise
    lower_wall = jnp.zeros_like(new_field[:, 0, :, 0, :])
    upper_wall = jnp.zeros_like(new_field[:, 0, :, 0, :])
    for offset in range(HALO + 1):
        lower_wall = lower_wall + wall_coef[0, offset] * new_field[:, 0, :, offset, :]
        upper_wall = (
            upper_wall + wall_coef[1, offset] * new_field[:, 0, :, row_count - 1 - offset, :]
        )
    wall_index = lax.axis_index("wall")
    wall_count = lax.axis_size("wall")
    lower_wall = jnp.where(wall_index == 0, lower_wall, 0.0 * lower_wall)
    upper_wall = jnp.where(wall_index == wall_count - 1, upper_wall, 0.0 * upper_wall)
    shear_rows = jnp.stack([lower_wall, upper_wall])
    onehot = (patch_of[:, None] == jnp.arange(PATCH, dtype=jnp.int32)[None, :]).astype(jnp.float32)
    partial_grad = jnp.einsum("wmcz,zp->wmcp", shear_rows, onehot, precision=lax.Precision.HIGHEST)
    wall_grad = lax.psum(partial_grad, ("wall", "span"))
    return (new_field, wall_grad)


def solution(mesh):
    return jax.shard_map(
        on_device,
        mesh=mesh,
        in_specs=(
            P(None, None, None, "wall", "span"),
            P(None, "wall"),
            P(None, "wall"),
            P(),
            P(),
            P("span"),
        ),
        out_specs=(P(None, None, None, "wall", "span"), P()),
        check_vma=False,
    )
```

profile of v0, /device:TPU:1, one launch (start us, length us, event | category | flops | bytes accessed | tf_op | source)
XLA Modules:
  0.0 284.4 jit_solution(1954556570748203936)
XLA Ops:
  0.6 3.2 %copy.115 = f32[4,3,2,32,384]{4,2,1,0,3:T(2,128)} copy(f32[4,3,2,32,384]{4,3,2,1,0:T(8,128)} %param.8) | data formatting | bytes 2359296 | tf_op args[0]
  3.8 11.7 %all-to-all-start = ((f32[12,2,32,384]{3,1,0,2:T(2,128)}), f32[12,2,32,384]{3,1,0,2:T(2,128)S(1)}, u32[]{:S(2)}, u32[]{:S(2)}) async-start(f32[12,2,32,384]{3,1,0,2:T(2,128)} %bitcast.18), calls=%async_computation | async-start | bytes 2359296 | tf_op jit(solution)/shard_map/all_to_all | solution.py:103
  15.6 0.8 copy.109
  16.3 0.9 fusion.198
  17.2 3.0 %collective-permute-start = (f32[4,3,2,7,384]{4,0,2,3,1:T(4,128)}, f32[4,3,2,7,384]{4,0,2,3,1:T(4,128)}, u32[]{:S(2)}, u32[]{:S(2)}) collective-permute-start(f32[4,3,2,7,384]{4,0,2,3,1:T(4,128)} %get-tuple-element.32), channel_id=1, source_target_pairs={{0,16},{16,32},{32,48},{48,64},{64,80},{80,96},{96,112},{112,128},... | collective-permute-start | bytes 774152 | tf_op jit(solution)/shard_map/ppermute | solution.py:19
  20.3 2.0 collective-permute-start.1
  22.3 0.7 fusion.83
  23.0 0.6 multiply_select_fusion
  23.6 21.4 %all-to-all-done = f32[12,2,32,384]{3,1,0,2:T(2,128)S(1)} async-done(((f32[12,2,32,384]{3,1,0,2:T(2,128)}), f32[12,2,32,384]{3,1,0,2:T(2,128)S(1)}, u32[]{:S(2)}, u32[]{:S(2)}) %all-to-all-start) | async-done | bytes 1179680 | tf_op jit(solution)/shard_map/all_to_all | solution.py:103
  45.0 1.4 copy.116
  46.4 2.1 all_to_all.27
  48.5 0.1 fusion.197
  48.6 0.5 reshape_squeeze.7
  49.1 0.8 fusion.77
  49.9 0.5 reshape_squeeze.6
  50.4 0.8 fusion.79
  51.1 0.8 convolution_add_fusion.3
  51.9 0.8 convolution_subtract_fusion.3
  52.7 0.9 fusion.24
  53.6 0.9 fusion.26
  54.5 0.9 fusion.4
  55.4 0.9 fusion.40
  56.3 0.9 fusion.5
  57.2 0.9 fusion.43
  58.0 0.9 convolution_subtract_fusion.1
  58.9 0.9 convolution_add_fusion.1
  59.8 0.8 fusion.32
  60.6 1.0 fusion.33
  61.7 0.8 fusion.3
  62.5 4.5 %copy.141 = f32[12,2,48,128]{0,1,3,2:T(2,128)} copy(f32[12,2,48,128]{3,2,1,0:T(8,128)S(1)} %fusion.3) | data formatting | bytes 1179648 | tf_op jit(solution)/shard_map/stack;reshape | solution.py:90
  67.0 1.6 fusion.1
  68.6 4.6 %copy.142 = f32[12,2,48,128]{0,1,3,2:T(2,128)} copy(f32[12,2,48,128]{3,2,1,0:T(8,128)S(1)} %fusion.1) | data formatting | bytes 1179648 | tf_op jit(solution)/shard_map/stack;reshape | solution.py:90
  73.2 11.8 %fusion.200 = f32[6144,2,2,12]{3,2,1,0:T(2,128)} fusion(f32[12,1,2,6144]{0,2,1,3:T(2,128)} %bitcast.155, f32[12,1,2,6144]{0,2,1,3:T(2,128)} %bitcast.154), kind=kLoop, calls=%fused_computation.261 | loop fusion | flops 294912 | bytes 2359296
  85.0 22.7 %reshape.465 = f32[16,1,18432]{2,1,0:T(1,128)} reshape(f32[6144,2,2,12]{3,2,1,0:T(2,128)} %fusion.200) | data formatting | bytes 2359296
  107.7 6.6 %all-to-all-start.1 = ((f32[16,1,18432]{2,1,0:T(1,128)}), f32[16,1,18432]{2,1,0:T(1,128)}, u32[]{:S(2)}, u32[]{:S(2)}) async-start(f32[16,1,18432]{2,1,0:T(1,128)} %reshape.465), calls=%async_computation.1 | async-start | bytes 2359296 | tf_op jit(solution)/shard_map/all_to_all | solution.py:105
  114.4 0.5 slice_bitcast_fusion.15
  114.9 0.1 fusion.139
  114.9 0.3 slice_multiply_fusion.15
  115.2 0.0 copy-start.9
  115.2 0.0 copy-start.8
  115.2 0.3 pad_maximum_fusion.1
  115.5 0.4 copy-done.9
  115.9 0.6 slice_bitcast_fusion.14
  116.5 0.7 fusion.199
  117.3 1.0 fusion.30
  118.3 0.0 collective-permute-done
  118.3 1.0 copy-done.3
  119.3 1.0 constant_dynamic-update-slice_fusion.1
  120.2 1.0 constant_dynamic-update-slice_fusion
  121.3 1.0 constant_dynamic-update-slice_fusion.2
  122.3 21.7 %all-to-all-done.1 = f32[16,1,18432]{2,1,0:T(1,128)} async-done(((f32[16,1,18432]{2,1,0:T(1,128)}), f32[16,1,18432]{2,1,0:T(1,128)}, u32[]{:S(2)}, u32[]{:S(2)}) %all-to-all-start.1) | async-done | bytes 1179680 | tf_op jit(solution)/shard_map/all_to_all | solution.py:105
  144.0 0.5 broadcast.394
  144.5 5.7 %reduce.2 = f32[16,18432]{1,0:T(8,128)} reduce(f32[16,1,18432]{2,1,0:T(1,128)} %all-to-all-done.1, f32[]{:T(128)} %broadcast.394), dimensions={1}, to_apply=%all_to_all.28.reduce_sub_computation | reduce | bytes 2359300 | tf_op jit(solution)/shard_map/all_to_all | solution.py:105
  150.2 27.5 %reshape.466 = f32[6144,2,2,12]{3,2,1,0:T(2,128)} reshape(f32[16,18432]{1,0:T(8,128)} %reduce.2) | data formatting | bytes 2359296
  177.7 11.2 %copy.143 = f32[12,2,2,16,384]{4,3,2,1,0:T(8,128)} copy(f32[12,2,2,16,384]{0,2,1,4,3:T(2,128)} %bitcast.153) | data formatting | bytes 2359296 | tf_op jit(solution)/shard_map/all_to_all | solution.py:105
  188.9 2.3 copy.124
  191.4 4.5 %fusion.8 = f32[4,3,2,32,384]{4,0,2,3,1:T(4,128)S(1)} fusion(f32[4,3,2,39,384]{4,0,2,3,1:T(4,128)S(1)} %constant_dynamic-update-slice_fusion.2, f32[4,3,2,39,384]{4,0,2,3,1:T(4,128)S(1)} %get-tuple-element.30, f32[4,3,2,32,384]{4,2,3,1,0:T(2,128)S(1)} %bitcast.156, f32[4,3,2,32,384]{4,0,2,3,1:T(4,128)S(1)} %copy-done.4, f32[32]{0:T(128)S(1)} %copy-done.19, ...), kind=kLoop, calls=%fused_computation.21 | loop fusion | flops 9732096 | bytes 21235584 | tf_op jit(solution)/shard_map/add | solution.py:116
  195.9 0.0 copy-start.22
  195.9 1.2 copy.126
  197.1 5.2 %multiply_select_fusion.1 = f32[1,4,2,384]{3,1,2,0:T(4,128)S(1)} fusion(f32[4,3,2,32,384]{4,0,2,3,1:T(4,128)S(1)} %fusion.8, f32[]{:T(128)} %bitcast.61, f32[]{:T(128)} %bitcast.60, f32[]{:T(128)} %bitcast.59, f32[]{:T(128)} %bitcast.58, f32[]{:T(128)} %bitcast.57, f32[]{:T(128)} %bitcast.56, f32[]{:T(128)} %bitcast.55, f32[]{:T(128)} %bitcast.54, pred[]{:T(512)S(6)} %eq.26), kind=kLoop, calls=%fused_computation.126 | loop fusion | flops 52224 | bytes 110625 | tf_op jit(solution)/shard_map/jit(_where)/select_n | solution.py:127
  202.4 5.1 %multiply_select_fusion.2 = f32[1,4,2,384]{3,1,2,0:T(4,128)S(1)} fusion(f32[4,3,2,32,384]{4,0,2,3,1:T(4,128)S(1)} %fusion.8, f32[]{:T(128)} %bitcast.52, f32[]{:T(128)} %bitcast.51, f32[]{:T(128)} %bitcast.50, f32[]{:T(128)} %bitcast.49, f32[]{:T(128)} %bitcast.48, f32[]{:T(128)} %bitcast.47, f32[]{:T(128)} %bitcast.46, f32[]{:T(128)} %bitcast.45, pred[]{:T(512)S(6)} %eq.25), kind=kLoop, calls=%fused_computation.127 | loop fusion | flops 52224 | bytes 110625 | tf_op jit(solution)/shard_map/jit(_where)/select_n | solution.py:126
  207.5 0.2 fusion.35
  207.7 76.1 %psum.7 = f32[2,4,2,64]{3,1,2,0:T(4,128)S(1)} all-reduce(f32[2,4,2,64]{3,1,2,0:T(4,128)S(1)} %fusion.35), channel_id=1, replica_groups=mesh['wall'=16,'span'=16] {'wall','span'}, use_global_device_ids=true, to_apply=%region_0.1 | all-reduce | flops 1024 | bytes 8192 | tf_op jit(solution)/shard_map/psum | solution.py:131
  283.8 0.6 copy.127
  (46 shorter events, 0.1 us)
Async XLA Ops:
  3.8 11.7 %copy-start = (f32[4,3,2,32,384]{4,3,2,1,0:T(8,128)S(1)}, f32[4,3,2,32,384]{4,3,2,1,0:T(8,128)}, u32[]{:S(2)}) copy-start(f32[4,3,2,32,384]{4,3,2,1,0:T(8,128)} %param.8) | copy-start | bytes 3538948
  3.8 41.2 %all-to-all-start = ((f32[12,2,32,384]{3,1,0,2:T(2,128)}), f32[12,2,32,384]{3,1,0,2:T(2,128)S(1)}, u32[]{:S(2)}, u32[]{:S(2)}) async-start(f32[12,2,32,384]{3,1,0,2:T(2,128)} %bitcast.18), calls=%async_computation | async-start | bytes 2359296 | tf_op jit(solution)/shard_map/all_to_all | solution.py:103
  17.2 101.0 %collective-permute-start = (f32[4,3,2,7,384]{4,0,2,3,1:T(4,128)}, f32[4,3,2,7,384]{4,0,2,3,1:T(4,128)}, u32[]{:S(2)}, u32[]{:S(2)}) collective-permute-start(f32[4,3,2,7,384]{4,0,2,3,1:T(4,128)} %get-tuple-element.32), channel_id=1, source_target_pairs={{0,16},{16,32},{32,48},{48,64},{64,80},{80,96},{96,112},{112,128},... | collective-permute-start | bytes 774152 | tf_op jit(solution)/shard_map/ppermute | solution.py:19
  20.3 101.0 %collective-permute-start.1 = (f32[4,3,2,7,384]{4,0,2,3,1:T(4,128)}, f32[4,3,2,7,384]{4,0,2,3,1:T(4,128)}, u32[]{:S(2)}, u32[]{:S(2)}) collective-permute-start(f32[4,3,2,7,384]{4,0,2,3,1:T(4,128)} %get-tuple-element.33), channel_id=1, source_target_pairs={{16,0},{32,16},{48,32},{64,48},{80,64},{96,80},{112,96},{128,112},... | collective-permute-start | bytes 774152 | tf_op jit(solution)/shard_map/ppermute | solution.py:22
  51.9 0.8 copy-start.5
  51.9 0.8 copy-start.6
  53.6 0.9 copy-start.7
  107.7 6.7 %copy-start.23 = (s32[4]{0:T(128)S(1)}, s32[4]{0:T(128)}, u32[]{:S(2)}) copy-start(s32[4]{0:T(128)} %param.12) | copy-start | bytes 52
  107.7 6.7 %copy-start.21 = (f32[2,32]{1,0:T(2,128)S(1)}, f32[2,32]{1,0:T(2,128)}, u32[]{:S(2)}) copy-start(f32[2,32]{1,0:T(2,128)} %param.9) | copy-start | bytes 772
  107.7 36.3 %all-to-all-start.1 = ((f32[16,1,18432]{2,1,0:T(1,128)}), f32[16,1,18432]{2,1,0:T(1,128)}, u32[]{:S(2)}, u32[]{:S(2)}) async-start(f32[16,1,18432]{2,1,0:T(1,128)} %reshape.465), calls=%async_computation.1 | async-start | bytes 2359296 | tf_op jit(solution)/shard_map/all_to_all | solution.py:105
  115.2 0.7 copy-start.9
  115.2 1.3 copy-start.8
  117.3 3.0 %copy-start.1 = (f32[4,3,2,32,384]{4,3,2,1,0:T(8,128)S(1)}, f32[4,3,2,32,384]{4,3,2,1,0:T(8,128)}, u32[]{:S(2)}) copy-start(f32[4,3,2,32,384]{4,3,2,1,0:T(8,128)} %param.8) | copy-start | bytes 3538948
  118.2 1.0 copy-start.3
  188.8 2.4 copy-start.2
  188.8 2.4 copy-start.4
  188.8 2.5 copy-start.10
  188.8 2.5 copy-start.11
  188.9 2.5 copy-start.12
  188.9 2.5 copy-start.13
  188.9 2.5 copy-start.14
  188.9 2.5 copy-start.15
  188.9 2.5 copy-start.16
  188.9 2.5 copy-start.17
  188.9 2.5 copy-start.18
  188.9 2.5 copy-start.19
  188.9 2.5 copy-start.20
  195.9 11.6 %copy-start.22 = (s32[384]{0:T(512)S(1)}, s32[384]{0:T(512)}, u32[]{:S(2)}) copy-start(s32[384]{0:T(512)} %param.13) | copy-start | bytes 4612
where the time goes:
time: 286 us; the launch traced here: 284 us
  local copies, waits for them, and re-layouts  90.8 us (32%)
  blocking collectives  76.1 us (27%)
  waiting for transfers between devices  43.1 us (15%)
  other arithmetic  35.3 us (12%)
  starting transfers between devices  23.4 us (8%)
  matrix products  14.5 us (5%)
    psum x1, blocking collectives, on_device(): wall_grad = lax.psum(partial_grad, ('wall', 'span'))  76.1 us
    unnamed x55, local copies, waits for them, and re-layouts  58.4 us
    all_to_all x1, waiting for transfers between devices, on_device(): lax.all_to_all(spectral_lines, 'span', split_axis=3, concat_axis=2, tiled...  21.7 us
    all_to_all x1, waiting for transfers between devices, on_device(): lax.all_to_all(flattened, 'span', split_axis=2, concat_axis=3, tiled=True)  21.4 us
    all_to_all x3, local copies, waits for them, and re-layouts, on_device(): lax.all_to_all(spectral_lines, 'span', split_axis=3, concat_axis=2, tiled...  14 us
    unnamed x1, other arithmetic  11.8 us
    all_to_all x1, starting transfers between devices, on_device(): lax.all_to_all(flattened, 'span', split_axis=2, concat_axis=3, tiled=True)  11.7 us
    another operation x2, local copies, waits for them, and re-layouts, spanwise_operator(): return jnp.stack([result_real, result_imag], axis=1)  9.1 us
  transfers between devices with their start and end apart: 4, of which 2 were waited for; matrix products, arithmetic and copies ran while one was open for 25% of the time, Pallas kernels for 0%

commit v1 on v0

--- a/solution.py
+++ b/solution.py
@@ -128,7 +128,7 @@
     shear_rows = jnp.stack([lower_wall, upper_wall])
     onehot = (patch_of[:, None] == jnp.arange(PATCH, dtype=jnp.int32)[None, :]).astype(jnp.float32)
     partial_grad = jnp.einsum("wmcz,zp->wmcp", shear_rows, onehot, precision=lax.Precision.HIGHEST)
-    wall_grad = lax.psum(partial_grad, ("wall", "span"))
+    wall_grad = lax.all_gather(partial_grad, ("wall", "span")).sum(axis=0)
     return (new_field, wall_grad)
 
 

time: 286 us -> 920 us (3.22)
  waiting for transfers between devices: 43.1 us -> 734 us
  blocking collectives: 76.1 us -> 0 us
  between operations: 1.24 us -> 14.6 us
    all_gather x0 -> x1, waiting for transfers between devices: none -> 691 us  [on_device(): wall_grad = lax.all_gather(partial_grad, ('wall', 'span')).sum(axis=0)]
    psum x1 -> x0, blocking collectives: 76.1 us -> none  [on_device(): wall_grad = lax.psum(partial_grad, ('wall', 'span'))]
    unnamed x55 -> x57, local copies, waits for them, and re-layouts: 58.4 us -> 59.7 us
  transfers between devices with their start and end apart: 4 -> 5, of which waited for: 2 -> 3; matrix products, arithmetic and copies ran while one was open for 25% -> 8% of each run, Pallas kernels for 0% -> 0%
where the time goes in v1:
time: 920 us; the launch traced here: 917 us
  waiting for transfers between devices  734 us (80%)
  local copies, waits for them, and re-layouts  92.1 us (10%)
  other arithmetic  37.3 us (4%)
  starting transfers between devices  23.4 us (3%)
  matrix products  15.1 us (2%)
  between operations  14.6 us (2%)
    all_gather x1, waiting for transfers between devices, on_device(): wall_grad = lax.all_gather(partial_grad, ('wall', 'span')).sum(axis=0)  691 us
    unnamed x57, local copies, waits for them, and re-layouts  59.7 us
    all_to_all x1, waiting for transfers between devices, on_device(): lax.all_to_all(spectral_lines, 'span', split_axis=3, concat_axis=2, tiled...  21.6 us
    all_to_all x1, waiting for transfers between devices, on_device(): lax.all_to_all(flattened, 'span', split_axis=2, concat_axis=3, tiled=True)  21.4 us
  transfers between devices with their start and end apart: 5, of which 3 were waited for; matrix products, arithmetic and copies ran while one was open for 8% of the time, Pallas kernels for 0%

profile of v1, /device:TPU:1, one launch (start us, length us, event | category | flops | bytes accessed | tf_op | source)
XLA Modules:
  0.0 916.5 jit_solution(1270246264563269594)
XLA Ops:
  7.2 3.2 copy.112
  10.4 11.7 %all-to-all-start = ((f32[12,2,32,384]{3,1,0,2:T(2,128)}), f32[12,2,32,384]{3,1,0,2:T(2,128)S(1)}, u32[]{:S(2)}, u32[]{:S(2)}) async-start(f32[12,2,32,384]{3,1,0,2:T(2,128)} %bitcast.18), calls=%async_computation | async-start | bytes 2359296 | tf_op jit(solution)/shard_map/all_to_all | solution.py:103
  22.1 0.8 copy.106
  22.9 0.9 fusion.198
  23.7 3.0 collective-permute-start
  26.8 1.9 collective-permute-start.1
  28.8 0.8 fusion.83
  29.5 0.6 multiply_select_fusion
  30.1 21.4 %all-to-all-done = f32[12,2,32,384]{3,1,0,2:T(2,128)S(1)} async-done(((f32[12,2,32,384]{3,1,0,2:T(2,128)}), f32[12,2,32,384]{3,1,0,2:T(2,128)S(1)}, u32[]{:S(2)}, u32[]{:S(2)}) %all-to-all-start) | async-done | bytes 1179680 | tf_op jit(solution)/shard_map/all_to_all | solution.py:103
  51.6 1.4 copy.113
  53.0 2.1 all_to_all.27
  55.1 0.1 fusion.197
  55.2 0.5 reshape_squeeze.7
  55.6 0.8 fusion.77
  56.4 0.5 reshape_squeeze.6
  56.9 0.8 fusion.79
  57.7 0.8 convolution_add_fusion.3
  58.5 0.8 convolution_subtract_fusion.3
  59.3 0.9 fusion.24
  60.2 0.9 fusion.26
  61.1 0.9 fusion.4
  61.9 0.9 fusion.40
  62.8 0.9 fusion.5
  63.7 0.9 fusion.43
  64.6 0.9 convolution_subtract_fusion.1
  65.5 0.9 convolution_add_fusion.1
  66.3 0.8 fusion.32
  67.2 1.0 fusion.33
  68.2 0.8 fusion.3
  69.1 4.5 copy.138
  73.5 1.6 fusion.1
  75.1 4.6 copy.139
  79.7 11.8 %fusion.200 = f32[6144,2,2,12]{3,2,1,0:T(2,128)} fusion(f32[12,1,2,6144]{0,2,1,3:T(2,128)} %bitcast.156, f32[12,1,2,6144]{0,2,1,3:T(2,128)} %bitcast.155), kind=kLoop, calls=%fused_computation.261 | loop fusion | flops 294912 | bytes 2359296
  91.5 22.7 %reshape.466 = f32[16,1,18432]{2,1,0:T(1,128)} reshape(f32[6144,2,2,12]{3,2,1,0:T(2,128)} %fusion.200) | data formatting | bytes 2359296
  114.2 6.6 all-to-all-start.1
  120.8 0.0 all-gather.3.cloned.1.call-start
  120.9 0.5 slice_bitcast_fusion.15
  121.4 0.1 fusion.139
  121.5 0.3 slice_multiply_fusion.15
  121.8 0.0 copy-start.9
  121.8 0.3 pad_maximum_fusion.1
  122.1 0.4 copy-done.10
  122.5 0.6 slice_bitcast_fusion.14
  123.1 0.7 fusion.199
  123.8 1.0 fusion.30
  124.8 1.0 copy-done.4
  125.8 1.0 constant_dynamic-update-slice_fusion.1
  126.8 1.0 constant_dynamic-update-slice_fusion
  127.9 1.0 constant_dynamic-update-slice_fusion.2
  128.9 21.6 %all-to-all-done.1 = f32[16,1,18432]{2,1,0:T(1,128)} async-done(((f32[16,1,18432]{2,1,0:T(1,128)}), f32[16,1,18432]{2,1,0:T(1,128)}, u32[]{:S(2)}, u32[]{:S(2)}) %all-to-all-start.1) | async-done | bytes 1179680 | tf_op jit(solution)/shard_map/all_to_all | solution.py:105
  150.5 0.5 broadcast.394
  151.0 5.7 reduce.2
  156.7 27.5 %reshape.467 = f32[6144,2,2,12]{3,2,1,0:T(2,128)} reshape(f32[16,18432]{1,0:T(8,128)} %reduce.2) | data formatting | bytes 2359296
  184.2 11.2 %copy.140 = f32[12,2,2,16,384]{4,3,2,1,0:T(8,128)} copy(f32[12,2,2,16,384]{0,2,1,4,3:T(2,128)} %bitcast.154) | data formatting | bytes 2359296 | tf_op jit(solution)/shard_map/all_to_all | solution.py:105
  195.5 2.3 copy.121
  197.9 4.5 fusion.8
  202.4 5.2 multiply_select_fusion.1
  207.6 5.1 multiply_select_fusion.2
  212.8 0.8 fusion.35
  213.5 0.0 all-gather.3.cloned.1.call-update
  213.6 2.5 copy.123
  216.1 690.9 %all-gather.3.cloned.1.call-done = f32[512,4,2,64]{3,1,2,0:T(4,128)} async-done(((f32[2,4,2,64]{3,1,2,0:T(4,128)}), f32[512,4,2,64]{3,1,2,0:T(4,128)}) %all-gather.3.cloned.1.call-update) | async-done | bytes 1048592 | tf_op jit(solution)/shard_map/all_gather | solution.py:131
  907.0 2.1 reduce_sum.9
  909.1 0.6 copy.124
  (51 shorter events, 0.1 us)
Async XLA Ops:
  10.4 11.7 %copy-start = (f32[4,3,2,32,384]{4,3,2,1,0:T(8,128)S(1)}, f32[4,3,2,32,384]{4,3,2,1,0:T(8,128)}, u32[]{:S(2)}) copy-start(f32[4,3,2,32,384]{4,3,2,1,0:T(8,128)} %param.8) | copy-start | bytes 3538948
  10.4 41.2 %all-to-all-start = ((f32[12,2,32,384]{3,1,0,2:T(2,128)}), f32[12,2,32,384]{3,1,0,2:T(2,128)S(1)}, u32[]{:S(2)}, u32[]{:S(2)}) async-start(f32[12,2,32,384]{3,1,0,2:T(2,128)} %bitcast.18), calls=%async_computation | async-start | bytes 2359296 | tf_op jit(solution)/shard_map/all_to_all | solution.py:103
  23.7 101.1 %collective-permute-start = (f32[4,3,2,7,384]{4,0,2,3,1:T(4,128)}, f32[4,3,2,7,384]{4,0,2,3,1:T(4,128)}, u32[]{:S(2)}, u32[]{:S(2)}) collective-permute-start(f32[4,3,2,7,384]{4,0,2,3,1:T(4,128)} %get-tuple-element.32), channel_id=1, source_target_pairs={{0,16},{16,32},{32,48},{48,64},{64,80},{80,96},{96,112},{112,128},... | collective-permute-start | bytes 774152 | tf_op jit(solution)/shard_map/ppermute | solution.py:19
  26.8 101.1 %collective-permute-start.1 = (f32[4,3,2,7,384]{4,0,2,3,1:T(4,128)}, f32[4,3,2,7,384]{4,0,2,3,1:T(4,128)}, u32[]{:S(2)}, u32[]{:S(2)}) collective-permute-start(f32[4,3,2,7,384]{4,0,2,3,1:T(4,128)} %get-tuple-element.33), channel_id=1, source_target_pairs={{16,0},{32,16},{48,32},{64,48},{80,64},{96,80},{112,96},{128,112},... | collective-permute-start | bytes 774152 | tf_op jit(solution)/shard_map/ppermute | solution.py:22
  58.5 0.8 copy-start.6
  58.5 0.8 copy-start.7
  60.2 0.9 copy-start.8
  114.2 6.7 copy-start.24
  114.2 6.7 copy-start.22
  114.2 36.3 %all-to-all-start.1 = ((f32[16,1,18432]{2,1,0:T(1,128)}), f32[16,1,18432]{2,1,0:T(1,128)}, u32[]{:S(2)}, u32[]{:S(2)}) async-start(f32[16,1,18432]{2,1,0:T(1,128)} %reshape.466), calls=%async_computation.1 | async-start | bytes 2359296 | tf_op jit(solution)/shard_map/all_to_all | solution.py:105
  120.8 786.1 %all-gather.3.cloned.1.call-start = ((), (), s32[]{:S(2)}) async-start(), calls=%async_computation.2 | async-start | bytes 2105344 | tf_op jit(solution)/shard_map/all_gather | solution.py:131
  121.8 0.7 copy-start.10
  121.8 1.3 copy-start.9
  123.8 3.0 copy-start.1
  124.8 1.0 copy-start.4
  195.4 2.4 copy-start.2
  195.4 2.4 copy-start.5
  195.4 2.5 copy-start.11
  195.4 2.5 copy-start.12
  195.4 2.5 copy-start.13
  195.4 2.5 copy-start.14
  195.4 2.5 copy-start.15
  195.4 2.5 copy-start.16
  195.4 2.5 copy-start.17
  195.4 2.5 copy-start.18
  195.4 2.5 copy-start.19
  195.4 2.5 copy-start.20
  195.4 2.5 copy-start.21
  197.9 14.8 %copy-start.23 = (s32[384]{0:T(512)S(1)}, s32[384]{0:T(512)}, u32[]{:S(2)}) copy-start(s32[384]{0:T(512)} %param.13) | copy-start | bytes 4612
  202.4 5.2 copy-start.3
Sparse Core Ops, SparseCore 0:
  213.7 693.2 all-gather.2
